TPU v7x, 32 devices: a whole 2x2x4 slice. The times are simulated.
32 devices in a mesh: inner: 4 (over y, x), outer: 8 (over z, core).
Axes of the slice: x: 2, y: 2, z: 4, core: 2. Of those that a mesh axis runs over, the one named last changes fastest.
Arguments:
- jac: float32 [512, 256, 256], P(('outer', 'inner')), may hold values from -0.5 to 1
- obs: float32 [512, 256], P(('outer', 'inner')), may hold values from -6 to 6
- gain_filter: float32 [256], replicated, may hold values from 0 to 0.1
- gain_smooth: float32 [256, 256], replicated, may hold values from -0.5 to 1
- init_mean: float32 [256], replicated, may hold values from -6 to 6
Outputs:
- filtered: float32 [512, 256], P(('outer', 'inner'))
- smoothed: float32 [512, 256], P(('outer', 'inner'))
All inputs are finite; a program needn't handle non-finite values.
Results may differ from a plain program's by a relative error of at most 0.0003.
Values sent between devices are 32-bit elements; how exact they have to be, the bound alone decides.
A program may use at most 64 MiB of HBM per device.

v0:
```python
import jax
import jax.numpy as jnp
from jax import lax
from jax.sharding import PartitionSpec as P

HIGHEST = lax.Precision.HIGHEST


def entering(part, axis, combine, identity):
    place = lax.axis_index(axis)
    gathered = lax.all_gather(part, axis)
    state = jnp.zeros_like(part) + jnp.asarray(identity, part.dtype)

    def one(turn, state):
        return combine(state, lax.dynamic_index_in_dim(gathered, turn, 0, False))

    return lax.fori_loop(0, place, one, state)


def last_row(state_width):
    return (jnp.arange(state_width + 1) == state_width).astype(jnp.float32)[:, None]


def identity_map(state_width):
    return jnp.concatenate(
        [jnp.eye(state_width, dtype=jnp.float32), jnp.zeros((1, state_width), jnp.float32)], 0
    )


def compose(earlier, later):
    state_width = later.shape[1]
    product = jnp.dot(earlier, later[:state_width], precision=HIGHEST)
    return product + last_row(state_width) * later[state_width][None, :]


def advance(packed, state):
    state_width = packed.shape[1]
    return jnp.dot(state, packed[:state_width], precision=HIGHEST) + packed[state_width]


def raise_power(factor, count):
    result = jnp.eye(factor.shape[0], dtype=jnp.float32)
    square = factor
    while count > 0:
        if count % 2 == 1:
            result = jnp.dot(result, square, precision=HIGHEST)
        count = count // 2
        if count > 0:
            square = jnp.dot(square, square, precision=HIGHEST)
    return result


def incoming_state(own_map, boundary):
    state_width = own_map.shape[1]
    identity = identity_map(state_width)
    inner_count = lax.axis_size("inner")
    inner_here = lax.axis_index("inner")
    gathered = lax.all_gather(own_map[None], "inner", axis=0, tiled=True)

    def absorb(running, inputs):
        before, group_total = running
        segment, position = inputs
        group_total = compose(group_total, segment)
        taken = position < inner_here
        before = jnp.where(taken, group_total, before)
        return ((before, group_total), None)

    (seg_before, group_total), _ = lax.scan(
        absorb,
        (identity, identity),
        (gathered, jnp.arange(inner_count, dtype=jnp.int32)),
        reverse=False,
    )
    group_before = entering(group_total, "outer", compose, identity)
    group_state = advance(group_before, boundary)
    return advance(seg_before, group_state)


def entering_backward(offset_sum, step_power):
    inner_count = lax.axis_size("inner")
    inner_here = lax.axis_index("inner")
    outer_count = lax.axis_size("outer")
    outer_here = lax.axis_index("outer")
    zero_state = jnp.zeros_like(offset_sum)
    seg_offsets = lax.all_gather(offset_sum[None], "inner", axis=0, tiled=True)

    def run_affine(power, here):

        def turn(running, inputs):
            state, caught = running
            offset, position = inputs
            caught = jnp.where(position == here, state, caught)
            state = jnp.dot(state, power, precision=HIGHEST) + offset
            return ((state, caught), None)

        return turn

    (group_offset, _), _ = lax.scan(
        run_affine(step_power, inner_here),
        (zero_state, zero_state),
        (seg_offsets, jnp.arange(inner_count, dtype=jnp.int32)),
        reverse=True,
    )
    group_power = raise_power(step_power, inner_count)
    group_offsets = lax.all_gather(group_offset[None], "outer", axis=0, tiled=True)
    (_, group_state), _ = lax.scan(
        run_affine(group_power, outer_here),
        (zero_state, zero_state),
        (group_offsets, jnp.arange(outer_count, dtype=jnp.int32)),
        reverse=True,
    )
    (_, device_state), _ = lax.scan(
        run_affine(step_power, inner_here),
        (group_state, group_state),
        (seg_offsets, jnp.arange(inner_count, dtype=jnp.int32)),
        reverse=True,
    )
    return device_state


def shards(jac, obs, gain_filter, gain_smooth, init_mean):
    state_width = jac.shape[1]
    step_count = jac.shape[0]
    retain = 1.0 - gain_filter
    bottom = last_row(state_width)

    def compose_forward(packed, inputs):
        step_matrix, measured = inputs
        moved = (
            lax.dot_general(packed, step_matrix, (((1,), (1,)), ((), ())), precision=HIGHEST)
            * retain[None, :]
        )
        return (moved + bottom * (gain_filter * measured)[None, :], None)

    forward_map, _ = lax.scan(compose_forward, identity_map(state_width), (jac, obs))
    start_state = incoming_state(forward_map, init_mean)

    def forward(state, inputs):
        step_matrix, measured = inputs
        predicted = jnp.dot(step_matrix, state, precision=HIGHEST)
        updated = predicted + gain_filter * (measured - predicted)
        return (updated, (predicted, updated))

    _, (predicted_all, filtered_all) = lax.scan(forward, start_state, (jac, obs))
    correction = filtered_all - predicted_all

    def backward(state, term):
        renewed = jnp.dot(gain_smooth, state, precision=HIGHEST) + term
        return (renewed, renewed)

    zero_state = jnp.zeros((state_width,), jnp.float32)
    offset_sum, _ = lax.scan(backward, zero_state, correction, reverse=True)
    step_power = raise_power(gain_smooth.T, step_count)
    after_state = entering_backward(offset_sum, step_power)
    _, back_states = lax.scan(backward, after_state, correction, reverse=True)
    return (filtered_all, predicted_all + back_states)


def solution(mesh):
    return jax.shard_map(
        shards,
        mesh=mesh,
        in_specs=(P(("outer", "inner"), None, None), P(("outer", "inner"), None), P(), P(), P()),
        out_specs=(P(("outer", "inner"), None), P(("outer", "inner"), None)),
        check_vma=False,
    )
```

profile of v0, /device:TPU:0, one launch (start us, length us, event | category | flops | bytes accessed | tf_op | source)
XLA Modules:
  0.0 221.8 jit_solution(6826046817942252627)
XLA Ops:
  8.0 34.7 %while.131 = (s32[]{:T(128)}, f32[257,256]{1,0:T(8,128)S(1)}, f32[16,256,256]{2,1,0:T(8,128)}, f32[256]{0:T(256)S(1)}, f32[256]{0:T(256)}, /*index=5*/f32[16,256]{1,0:T(8,128)}, s32[]{:T(128)}) while((s32[]{:T(128)}, f32[257,256]{1,0:T(8,128)S(1)}, f32[16,256,256]{2,1,0:T(8,128)}, f32[256]{0:T(256)S(1)}, f32[256]{0:T(256)}, ...), condition=%wide.region_1.2_spmd.clone, body=%wide.region_0.1_spmd.clone.sunk | while | flops 202311168 | bytes 1322585 | solution.py:135
  8.8 1.4 fusion.109
  10.9 1.4 fusion.109
  15.3 1.4 fusion.109
  19.6 1.4 fusion.109
  23.9 1.4 fusion.109
  28.3 1.4 fusion.109
  32.6 1.4 fusion.109
  37.0 1.4 fusion.109
  41.3 1.4 fusion.109
  43.5 29.5 %all-gather.11.cloned.1.call-done = f32[4,257,256]{2,1,0:T(8,128)} async-done(((f32[1,257,256]{2,1,0:T(8,128)}), f32[4,257,256]{2,1,0:T(8,128)}) %all-gather.11.cloned.1.call-update) | async-done | bytes 1052688 | tf_op jit(solution)/shard_map/all_gather | solution.py:58
  73.1 14.0 %while.126 = (s32[]{:T(128)}, f32[257,256]{1,0:T(8,128)S(1)}, f32[257,256]{1,0:T(8,128)S(1)}, s32[4]{0:T(128)S(1)}, s32[]{:T(128)}, /*index=5*/f32[4,257,256]{2,1,0:T(8,128)}, s32[]{:T(128)}, s32[]{:T(128)}, s32[]{}) while((s32[]{:T(128)}, f32[257,256]{1,0:T(8,128)S(1)}, f32[257,256]{1,0:T(8,128)S(1)}, s32[4]{0:T(128)S(1)}, s32[]{:T(128)}, ...), condition=%wide.region_3.4_spmd, body=%wide.region_2.3_spmd.sunk | while | flops 202310912 | bytes 1846927 | solution.py:68
  75.1 1.5 broadcast_select_fusion.9
  78.6 1.5 broadcast_select_fusion.9
  82.1 1.5 broadcast_select_fusion.9
  85.6 1.5 broadcast_select_fusion.9
  91.0 26.7 %all-gather.13.cloned.1.call-done = f32[8,257,256]{2,1,0:T(8,128)} async-done(((f32[1,257,256]{2,1,0:T(8,128)}), f32[8,257,256]{2,1,0:T(8,128)}) %all-gather.13.cloned.1.call-update) | async-done | bytes 2105360 | tf_op jit(solution)/shard_map/all_gather | solution.py:11
  118.3 33.3 %while.128 = (s32[]{:T(128)}, f32[256]{0:T(256)S(1)}, f32[16,256]{1,0:T(8,128)S(1)}, f32[16,256]{1,0:T(8,128)S(1)}, f32[16,256,256]{2,1,0:T(8,128)}, /*index=5*/...) while((s32[]{:T(128)}, f32[256]{0:T(256)S(1)}, f32[16,256]{1,0:T(8,128)S(1)}, ...), condition=%wide.region_7.8_spmd, body=%wide.region_6.7_spmd.sunk | while | flops 787202 | bytes 275049 | solution.py:144
  151.6 6.1 %while.132 = (s32[]{:T(128)}, f32[256]{0:T(256)S(1)}, f32[256,256]{1,0:T(8,128)S(1)}, f32[16,256]{1,0:T(8,128)S(1)}, s32[]{:T(128)}, /*index=5*/s32[]{:T(128)}, s32[]{:T(128)}) while((s32[]{:T(128)}, f32[256]{0:T(256)S(1)}, f32[256,256]{1,0:T(8,128)S(1)}, f32[16,256]{1,0:T(8,128)S(1)}, s32[]{:T(128)}, /*index=5*/s32[]{:T(128)}, ...), condition=%wide.region_9.10_spmd.clone, body=%wide.region_8.9_spmd.clone.sunk | while | flops 786948 | bytes 271463 | solution.py:152
  157.7 8.0 %all-gather.6 = f32[4,1,256]{2,1,0:T(1,128)S(1)} all-gather(f32[1,1,256]{2,1,0:T(1,128)S(1)} %bitcast.222), channel_id=4, replica_groups=mesh['inner'=4,'outer'=8] {'inner'}, dimensions={0}, use_global_device_ids=true | all-gather | bytes 5120 | tf_op jit(solution)/shard_map/all_gather | solution.py:85
  166.9 22.8 %all-gather.7 = f32[8,1,256]{2,1,0:T(1,128)S(1)} all-gather(f32[1,1,256]{2,1,0:T(1,128)S(1)} %bitcast.221), channel_id=5, replica_groups=mesh['inner'=4,'outer'=8] {'outer'}, dimensions={0}, use_global_device_ids=true | all-gather | bytes 9216 | tf_op jit(solution)/shard_map/all_gather | solution.py:105
  189.7 12.2 %while.134 = (s32[]{:T(128)}, f32[256]{0:T(256)S(1)}, f32[256]{0:T(256)S(1)}, f32[256,256]{1,0:T(8,128)S(1)}, f32[8,256]{1,0:T(8,128)S(1)}, /*index=5*/s32[8]{0:...) while((s32[]{:T(128)}, f32[256]{0:T(256)S(1)}, f32[256]{0:T(256)S(1)}, ...), condition=%wide.region_13.14_spmd.clone, body=%wide.region_12.13_spmd.clone.sunk | while | flops 787461 | bytes 273557 | solution.py:106
  201.9 6.0 %while.129 = (s32[]{:T(128)}, f32[256]{0:T(256)S(1)}, f32[256]{0:T(256)S(1)}, f32[256,256]{1,0:T(8,128)S(1)}, f32[4,256]{1,0:T(4,128)S(1)}, /*index=5*/s32[4]{0:T(128)S(1)}, s32[]{:T(128)}, s32[]{:T(128)}, s32[]{:T(128)}) while((s32[]{:T(128)}, f32[256]{0:T(256)S(1)}, f32[256]{0:T(256)S(1)}, f32[256,256]{1,0:T(8,128)S(1)}, ...), condition=%wide.region_15.16_spmd, body=%wide.region_14.15_spmd.sunk | while | flops 786948 | bytes 272515 | solution.py:112
  207.9 6.3 %while.130 = (s32[]{:T(128)}, f32[256]{0:T(256)S(1)}, f32[16,256]{1,0:T(8,128)S(1)}, f32[256,256]{1,0:T(8,128)S(1)}, f32[16,256]{1,0:T(8,128)S(1)}, /*index=5*/s32[]{:T(128)}, s32[]{:T(128)}, s32[]{:T(128)}) while((s32[]{:T(128)}, f32[256]{0:T(256)S(1)}, f32[16,256]{1,0:T(8,128)S(1)}, f32[256,256]{1,0:T(8,128)S(1)}, ...), condition=%wide.region_17.18_spmd, body=%wide.region_16.17_spmd.sunk | while | flops 786691 | bytes 271465 | solution.py:155
  (408 shorter events, 90.1 us)
Async XLA Ops:
  7.2 110.5 %copy-start = (f32[256]{0:T(256)S(1)}, f32[256]{0:T(256)}, u32[]{:S(2)}) copy-start(f32[256]{0:T(256)} %param.27) | copy-start | bytes 3076
  7.2 65.9 %all-gather.11.cloned.1.call-start = ((), (), s32[]{:S(2)}) async-start(), calls=%async_computation | async-start | bytes 1351680 | tf_op jit(solution)/shard_map/all_gather | solution.py:58
  42.7 0.7 copy-start.3
  43.4 74.2 %all-gather.13.cloned.1.call-start = ((), (), s32[]{:S(2)}) async-start(), calls=%async_computation.1 | async-start | bytes 2433024 | tf_op jit(solution)/shard_map/all_gather | solution.py:11
  73.1 14.8 %copy-start.1 = (f32[256,256]{1,0:T(8,128)S(1)}, f32[256,256]{1,0:T(8,128)}, u32[]{:S(2)}) copy-start(f32[256,256]{1,0:T(8,128)} %param.26) | copy-start | bytes 786436
  87.1 0.7 copy-start.2
  117.6 0.7 copy-start.4
  151.6 38.1 %copy-start.5 = (f32[16,256]{1,0:T(8,128)}, f32[16,256]{1,0:T(8,128)S(1)}, u32[]{:S(2)}) copy-start(f32[16,256]{1,0:T(8,128)S(1)} %get-tuple-element.684) | copy-start | bytes 49156
Sparse Core Ops, SparseCore 0:
  43.5 29.4 all-gather.10
  87.9 29.6 all-gather.12
where the time goes:
time: 225 us; the launch traced here: 222 us
  matrix products  62.5 us (28%)
  waiting for transfers between devices  56.2 us (25%)
  blocking collectives  30.9 us (14%)
  local copies, waits for them, and re-layouts  30.6 us (14%)
  between operations  14.4 us (6%)
  other arithmetic  14.1 us (6%)
  loops' own time  13 us (6%)
    all_gather x1, waiting for transfers between devices, incoming_state(): gathered = lax.all_gather(own_map[None], 'inner', axis=0, tiled=True)  29.5 us
    all_gather x1, waiting for transfers between devices, entering(): gathered = lax.all_gather(part, axis)  26.7 us
    all_gather x1, blocking collectives, entering_backward(): lax.all_gather(group_offset[None], 'outer', axis=0, tiled=True)  22.8 us
    dot_general x16, matrix products, compose_forward(): lax.dot_general(packed, step_matrix, (((1,), (1,)), ((), ())), precision=...  21.9 us
    dot_general x16, matrix products, forward(): predicted = jnp.dot(step_matrix, state, precision=HIGHEST)  19.5 us
    dynamic_slice x48, local copies, waits for them, and re-layouts, shards(): lax.scan(compose_forward, identity_map(state_width), (jac, obs))  13.3 us
    mul x16, other arithmetic, compose_forward(): return (moved + bottom * (gain_filter * measured)[None, :], None)  11.6 us
    dot_general x32, matrix products, backward(): renewed = jnp.dot(gain_smooth, state, precision=HIGHEST) + term  8.65 us
  transfers between devices with their start and end apart: 2, of which 2 were waited for; matrix products, arithmetic and copies ran while one was open for 1% of the time, Pallas kernels for 0%

commit v1 on v0

--- a/solution.py
+++ b/solution.py
@@ -55,7 +55,9 @@
     identity = identity_map(state_width)
     inner_count = lax.axis_size("inner")
     inner_here = lax.axis_index("inner")
-    gathered = lax.all_gather(own_map[None], "inner", axis=0, tiled=True)
+    block = own_map[None]
+    sent = jnp.stack([block] * lax.axis_size("inner"))
+    gathered = jnp.concatenate(lax.all_to_all(sent, "inner", 0, 0), axis=0)
 
     def absorb(running, inputs):
         before, group_total = running

time: 225 us -> 209 us (0.929)
  waiting for transfers between devices: 56.2 us -> 40.6 us
  starting transfers between devices: 0.08 us -> 5.19 us
  matrix products: 62.5 us -> 58.8 us
    all_gather x1 -> x0, waiting for transfers between devices: 29.5 us -> none  [incoming_state(): gathered = lax.all_gather(own_map[None], 'inner', axis=0, tiled=True)]
    all_to_all x0 -> x1, waiting for transfers between devices: none -> 13.6 us  [incoming_state(): gathered = jnp.concatenate(lax.all_to_all(sent, 'inner', 0, 0), axis=0)]
    all_to_all x0 -> x1, starting transfers between devices: none -> 5.19 us  [incoming_state(): gathered = jnp.concatenate(lax.all_to_all(sent, 'inner', 0, 0), axis=0)]
    dot_general x4, matrix products: 5.96 us -> 2.19 us  [compose(): product = jnp.dot(earlier, later[:state_width], precision=HIGHEST)]
    slice x4, local copies, waits for them, and re-layouts: 2.85 us -> 0.04 us  [compose(): return product + last_row(state_width) * later[state_width][None, :]]
  transfers between devices with their start and end apart: 2 -> 2, of which waited for: 2 -> 2; matrix products, arithmetic and copies ran while one was open for 1% -> 2% of each run, Pallas kernels for 0% -> 0%
where the time goes in v1:
time: 209 us; the launch traced here: 206 us
  matrix products  58.8 us (28%)
  waiting for transfers between devices  40.6 us (19%)
  blocking collectives  30.9 us (15%)
  local copies, waits for them, and re-layouts  28.7 us (14%)
  between operations  14.4 us (7%)
  other arithmetic  14.1 us (7%)
  loops' own time  13.1 us (6%)
  starting transfers between devices  5.19 us (2%)
    all_gather x1, waiting for transfers between devices, entering(): gathered = lax.all_gather(part, axis)  27 us
    all_gather x1, blocking collectives, entering_backward(): lax.all_gather(group_offset[None], 'outer', axis=0, tiled=True)  22.8 us
    dot_general x16, matrix products, compose_forward(): lax.dot_general(packed, step_matrix, (((1,), (1,)), ((), ())), precision=...  21.9 us
    dot_general x16, matrix products, forward(): predicted = jnp.dot(step_matrix, state, precision=HIGHEST)  19.5 us
    all_to_all x1, waiting for transfers between devices, incoming_state(): gathered = jnp.concatenate(lax.all_to_all(sent, 'inner', 0, 0), axis=0)  13.6 us
    dynamic_slice x48, local copies, waits for them, and re-layouts, shards(): lax.scan(compose_forward, identity_map(state_width), (jac, obs))  13.3 us
    mul x16, other arithmetic, compose_forward(): return (moved + bottom * (gain_filter * measured)[None, :], None)  11.6 us
    dot_general x32, matrix products, backward(): renewed = jnp.dot(gain_smooth, state, precision=HIGHEST) + term  8.65 us
  transfers between devices with their start and end apart: 2, of which 2 were waited for; matrix products, arithmetic and copies ran while one was open for 2% of the time, Pallas kernels for 0%

profile of v1, /device:TPU:0, one launch (start us, length us, event | category | flops | bytes accessed | tf_op | source)
XLA Modules:
  0.0 205.7 jit_solution(2330421047805529331)
XLA Ops:
  8.0 34.7 %while.131 = (s32[]{:T(128)}, f32[257,256]{1,0:T(8,128)S(1)}, f32[16,256,256]{2,1,0:T(8,128)}, f32[256]{0:T(256)S(1)}, f32[256]{0:T(256)}, /*index=5*/f32[16,256]{1,0:T(8,128)}, s32[]{:T(128)}) while((s32[]{:T(128)}, f32[257,256]{1,0:T(8,128)S(1)}, f32[16,256,256]{2,1,0:T(8,128)}, f32[256]{0:T(256)S(1)}, f32[256]{0:T(256)}, ...), condition=%wide.region_1.2_spmd.clone, body=%wide.region_0.1_spmd.clone.sunk | while | flops 202311168 | bytes 1322585 | solution.py:137
  8.7 1.4 fusion.109
  13.1 1.4 fusion.109
  15.2 1.4 fusion.109
  17.4 1.4 fusion.109
  21.7 1.4 fusion.109
  23.9 1.4 fusion.109
  26.1 1.4 fusion.109
  30.4 1.4 fusion.109
  32.6 1.4 fusion.109
  34.7 1.4 fusion.109
  39.1 1.4 fusion.109
  42.6 1.5 stack.3
  44.2 5.2 %all-to-all-start = ((f32[4,1,257,256]{3,1,2,0:T(1,128)}), f32[4,1,257,256]{3,1,2,0:T(1,128)S(1)}, u32[]{:S(2)}, u32[]{:S(2)}) async-start(f32[4,1,257,256]{3,1,2,0:T(1,128)} %stack.3), calls=%async_computation | async-start | bytes 2105344 | tf_op jit(solution)/shard_map/all_to_all | solution.py:60
  49.4 13.6 %all-to-all-done = f32[4,1,257,256]{3,1,2,0:T(1,128)S(1)} async-done(((f32[4,1,257,256]{3,1,2,0:T(1,128)}), f32[4,1,257,256]{3,1,2,0:T(1,128)S(1)}, u32[]{:S(2)}, u32[]{:S(2)}) %all-to-all-start) | async-done | bytes 1052704 | tf_op jit(solution)/shard_map/all_to_all | solution.py:60
  63.2 7.5 %while.126 = (s32[]{:T(128)}, f32[257,256]{1,0:T(8,128)S(1)}, f32[257,256]{1,0:T(8,128)S(1)}, s32[4]{0:T(128)S(1)}, s32[]{:T(128)}, /*index=5*/f32[4,257,256]{2,1,0:T(8,128)S(1)}, s32[]{:T(128)}, s32[]{:T(128)}, s32[]{}) while((s32[]{:T(128)}, f32[257,256]{1,0:T(8,128)S(1)}, f32[257,256]{1,0:T(8,128)S(1)}, s32[4]{0:T(128)S(1)}, s32[]{:T(128)}, ...), condition=%wide.region_3.4_spmd, body=%wide.region_2.3_spmd.sunk | while | flops 202310912 | bytes 1861775 | solution.py:70
  74.6 27.0 %all-gather.8.cloned.1.call-done = f32[8,257,256]{2,1,0:T(8,128)} async-done(((f32[1,257,256]{2,1,0:T(8,128)}), f32[8,257,256]{2,1,0:T(8,128)}) %all-gather.8.cloned.1.call-update) | async-done | bytes 2105360 | tf_op jit(solution)/shard_map/all_gather | solution.py:11
  102.2 33.3 %while.128 = (s32[]{:T(128)}, f32[256]{0:T(256)S(1)}, f32[16,256]{1,0:T(8,128)S(1)}, f32[16,256]{1,0:T(8,128)S(1)}, f32[16,256,256]{2,1,0:T(8,128)}, /*index=5*/...) while((s32[]{:T(128)}, f32[256]{0:T(256)S(1)}, f32[16,256]{1,0:T(8,128)S(1)}, ...), condition=%wide.region_7.8_spmd, body=%wide.region_6.7_spmd.sunk | while | flops 787202 | bytes 275049 | solution.py:146
  135.6 6.1 %while.132 = (s32[]{:T(128)}, f32[256]{0:T(256)S(1)}, f32[256,256]{1,0:T(8,128)S(1)}, f32[16,256]{1,0:T(8,128)S(1)}, s32[]{:T(128)}, /*index=5*/s32[]{:T(128)}, s32[]{:T(128)}) while((s32[]{:T(128)}, f32[256]{0:T(256)S(1)}, f32[256,256]{1,0:T(8,128)S(1)}, f32[16,256]{1,0:T(8,128)S(1)}, s32[]{:T(128)}, /*index=5*/s32[]{:T(128)}, ...), condition=%wide.region_9.10_spmd.clone, body=%wide.region_8.9_spmd.clone.sunk | while | flops 786948 | bytes 271463 | solution.py:154
  141.7 8.0 %all-gather.4 = f32[4,1,256]{2,1,0:T(1,128)S(1)} all-gather(f32[1,1,256]{2,1,0:T(1,128)S(1)} %bitcast.224), channel_id=3, replica_groups=mesh['inner'=4,'outer'=8] {'inner'}, dimensions={0}, use_global_device_ids=true | all-gather | bytes 5120 | tf_op jit(solution)/shard_map/all_gather | solution.py:87
  150.8 22.8 %all-gather.5 = f32[8,1,256]{2,1,0:T(1,128)S(1)} all-gather(f32[1,1,256]{2,1,0:T(1,128)S(1)} %bitcast.223), channel_id=4, replica_groups=mesh['inner'=4,'outer'=8] {'outer'}, dimensions={0}, use_global_device_ids=true | all-gather | bytes 9216 | tf_op jit(solution)/shard_map/all_gather | solution.py:107
  173.6 12.2 %while.134 = (s32[]{:T(128)}, f32[256]{0:T(256)S(1)}, f32[256]{0:T(256)S(1)}, f32[256,256]{1,0:T(8,128)S(1)}, f32[8,256]{1,0:T(8,128)S(1)}, /*index=5*/s32[8]{0:...) while((s32[]{:T(128)}, f32[256]{0:T(256)S(1)}, f32[256]{0:T(256)S(1)}, ...), condition=%wide.region_13.14_spmd.clone, body=%wide.region_12.13_spmd.clone.sunk | while | flops 787461 | bytes 273557 | solution.py:108
  185.8 6.0 %while.129 = (s32[]{:T(128)}, f32[256]{0:T(256)S(1)}, f32[256]{0:T(256)S(1)}, f32[256,256]{1,0:T(8,128)S(1)}, f32[4,256]{1,0:T(4,128)S(1)}, /*index=5*/s32[4]{0:T(128)S(1)}, s32[]{:T(128)}, s32[]{:T(128)}, s32[]{:T(128)}) while((s32[]{:T(128)}, f32[256]{0:T(256)S(1)}, f32[256]{0:T(256)S(1)}, f32[256,256]{1,0:T(8,128)S(1)}, ...), condition=%wide.region_15.16_spmd, body=%wide.region_14.15_spmd.sunk | while | flops 786948 | bytes 272515 | solution.py:114
  191.9 6.3 %while.130 = (s32[]{:T(128)}, f32[256]{0:T(256)S(1)}, f32[16,256]{1,0:T(8,128)S(1)}, f32[256,256]{1,0:T(8,128)S(1)}, f32[16,256]{1,0:T(8,128)S(1)}, /*index=5*/s32[]{:T(128)}, s32[]{:T(128)}, s32[]{:T(128)}) while((s32[]{:T(128)}, f32[256]{0:T(256)S(1)}, f32[16,256]{1,0:T(8,128)S(1)}, f32[256,256]{1,0:T(8,128)S(1)}, ...), condition=%wide.region_17.18_spmd, body=%wide.region_16.17_spmd.sunk | while | flops 786691 | bytes 271465 | solution.py:157
  (407 shorter events, 86.1 us)
Async XLA Ops:
  7.2 94.4 %copy-start = (f32[256]{0:T(256)S(1)}, f32[256]{0:T(256)}, u32[]{:S(2)}) copy-start(f32[256]{0:T(256)} %param.27) | copy-start | bytes 3076
  44.2 18.9 %all-to-all-start = ((f32[4,1,257,256]{3,1,2,0:T(1,128)}), f32[4,1,257,256]{3,1,2,0:T(1,128)S(1)}, u32[]{:S(2)}, u32[]{:S(2)}) async-start(f32[4,1,257,256]{3,1,2,0:T(1,128)} %stack.3), calls=%async_computation | async-start | bytes 2105344 | tf_op jit(solution)/shard_map/all_to_all | solution.py:60
  49.4 52.2 %all-gather.8.cloned.1.call-start = ((), (), s32[]{:S(2)}) async-start(), calls=%async_computation.1 | async-start | bytes 2433024 | tf_op jit(solution)/shard_map/all_gather | solution.py:11
  63.2 8.3 %copy-start.1 = (f32[256,256]{1,0:T(8,128)S(1)}, f32[256,256]{1,0:T(8,128)}, u32[]{:S(2)}) copy-start(f32[256,256]{1,0:T(8,128)} %param.26) | copy-start | bytes 786436
  70.7 0.7 copy-start.2
  101.6 0.7 copy-start.3
  135.6 38.1 %copy-start.4 = (f32[16,256]{1,0:T(8,128)}, f32[16,256]{1,0:T(8,128)S(1)}, u32[]{:S(2)}) copy-start(f32[16,256]{1,0:T(8,128)S(1)} %get-tuple-element.684) | copy-start | bytes 49156
Sparse Core Ops, SparseCore 0:
  71.5 30.0 all-gather.7
